TPU v7x, 32 devices: a whole 2x2x4 slice. The times are simulated.
32 devices in a mesh: dp: 4 (over y, x), fsdp: 8 (over z, core).
Axes of the slice: x: 2, y: 2, z: 4, core: 2. Of those that a mesh axis runs over, the one named last changes fastest.
Arguments:
- tokens: bfloat16 [4096, 1536], P(('dp', 'fsdp')), may hold values from -6 to 6
- lengths: int32 [32], P(('dp', 'fsdp')), may hold values from 64 to 128, as said below
- positions: int32 [4096], P(('dp', 'fsdp')), may hold values from 0 to 4476, as said below
- conditioning: bfloat16 [4096, 768], P(('dp', 'fsdp')), may hold values from -6 to 6
- gain_one: bfloat16 [1536], P(('dp', 'fsdp')), may hold values from 0.5 to 1.5
- self_proj: bfloat16 [1536, 4608], P(('dp', 'fsdp')), may hold values from -0.15625 to 0.15625
- self_out: bfloat16 [1536, 1536], P(('dp', 'fsdp')), may hold values from -1.25 to 1.25
- gain_two: bfloat16 [1536], P(('dp', 'fsdp')), may hold values from 0.5 to 1.5
- cross_query: bfloat16 [1536, 1536], P(('dp', 'fsdp')), may hold values from -0.15625 to 0.15625
- cross_keyval: bfloat16 [768, 3072], P(('dp', 'fsdp')), may hold values from -0.21875 to 0.21875
- cross_out: bfloat16 [1536, 1536], P(('dp', 'fsdp')), may hold values from -0.875 to 0.875
- gain_three: bfloat16 [1536], P(('dp', 'fsdp')), may hold values from 0.5 to 1.5
- feed_in: bfloat16 [1536, 12288], P(('dp', 'fsdp')), may hold values from -0.15625 to 0.15625
- feed_bias: bfloat16 [12288], P(('dp', 'fsdp')), may hold values from -3 to 3
- feed_down: bfloat16 [6144, 1536], P(('dp', 'fsdp')), may hold values from -0.078125 to 0.078125
- down_bias: bfloat16 [1536], P(('dp', 'fsdp')), may hold values from -3 to 3
- cotangent: bfloat16 [4096, 1536], P(('dp', 'fsdp')), may hold values from -6 to 6
Outputs:
- output: bfloat16 [4096, 1536], P(('dp', 'fsdp'))
- tokens_grad: float32 [4096, 1536], P(('dp', 'fsdp'))
- gain_one_grad: float32 [1536], P(('dp', 'fsdp'))
- self_proj_grad: float32 [1536, 4608], P(('dp', 'fsdp'))
- self_out_grad: float32 [1536, 1536], P(('dp', 'fsdp'))
- gain_two_grad: float32 [1536], P(('dp', 'fsdp'))
- cross_query_grad: float32 [1536, 1536], P(('dp', 'fsdp'))
- cross_keyval_grad: float32 [768, 3072], P(('dp', 'fsdp'))
- cross_out_grad: float32 [1536, 1536], P(('dp', 'fsdp'))
- gain_three_grad: float32 [1536], P(('dp', 'fsdp'))
- feed_in_grad: float32 [1536, 12288], P(('dp', 'fsdp'))
- feed_bias_grad: float32 [12288], P(('dp', 'fsdp'))
- feed_down_grad: float32 [6144, 1536], P(('dp', 'fsdp'))
- down_bias_grad: float32 [1536], P(('dp', 'fsdp'))
Inputs may be any that keep to these rules, and one draw needn't show every extreme that they name: `lengths`: each item's length is 64 or 128, and both occur. Within an item the positions rise from its first slot by a fixed stride of 1, 2 or 3.
All inputs are finite; a program needn't handle non-finite values.
Results may differ from a plain program's by a relative error of at most 0.022.
Values may be sent and summed in bfloat16 or wider, within the bound.
No kernel may reach another device: no remote copies, remote signals or barrier semaphores. Data moves between devices by JAX's collectives and lax.ppermute only.
A program may use at most 704 MiB of HBM per device.

v0:
```python
import jax
import jax.numpy as jnp
from jax import lax
from jax.sharding import PartitionSpec as P

HEADS = 24
HD = 64


def norm_rows(v, gain):
    centre = v - jnp.mean(v, axis=-1, keepdims=True)
    rstd = lax.rsqrt(jnp.mean(centre * centre, axis=-1, keepdims=True) + 1e-05)
    unit = centre * rstd
    return (unit * gain, unit, rstd)


def norm_back(grad, gain, unit, rstd):
    scaled = grad * gain
    back = rstd * (
        scaled
        - jnp.mean(scaled, axis=-1, keepdims=True)
        - unit * jnp.mean(scaled * unit, axis=-1, keepdims=True)
    )
    return (back, jnp.sum(grad * unit, axis=0))


def outer_sum(left, right):
    return lax.dot_general(
        left, right, (((0,), (0,)), ((), ())), preferred_element_type=jnp.float32
    )


def back_mul(grad, weight):
    return lax.dot_general(
        grad, weight, (((1,), (1,)), ((), ())), preferred_element_type=jnp.float32
    )


def rotate(t, cosine, sine):
    quarter = cosine.shape[-1]
    first = t[..., :quarter]
    second = t[..., quarter : 2 * quarter]
    return jnp.concatenate(
        [first * cosine - second * sine, second * cosine + first * sine, t[..., 2 * quarter :]],
        axis=-1,
    )


def raw_scores(query, keys, mask):
    scores = jnp.einsum("qhd,khd->hqk", query, keys, preferred_element_type=jnp.float32) * 0.125
    if mask is not None:
        scores = jnp.where(mask, scores, -1e30)
    return scores


def attend(query, keys, values, mask):
    scores = raw_scores(query, keys, mask)
    top = jnp.max(scores, axis=-1, keepdims=True)
    weight = jnp.exp(scores - top)
    total = jnp.sum(weight, axis=-1, keepdims=True)
    probs = (weight / total).astype(jnp.bfloat16)
    result = jnp.einsum("hqk,khd->qhd", probs, values, preferred_element_type=jnp.float32)
    return (result, top + jnp.log(total))


def attend_back(query, keys, values, mask, lse, grad_out):
    probs = jnp.exp(raw_scores(query, keys, mask) - lse)
    dprob = jnp.einsum("qhd,khd->hqk", grad_out, values, preferred_element_type=jnp.float32)
    dvalues = jnp.einsum(
        "hqk,qhd->khd", probs.astype(jnp.bfloat16), grad_out, preferred_element_type=jnp.float32
    )
    delta = jnp.sum(dprob * probs, axis=-1, keepdims=True)
    dscore = (probs * (dprob - delta)).astype(jnp.bfloat16)
    dquery = jnp.einsum("hqk,khd->qhd", dscore, keys, preferred_element_type=jnp.float32) * 0.125
    dkeys = jnp.einsum("hqk,qhd->khd", dscore, query, preferred_element_type=jnp.float32) * 0.125
    return (dquery, dkeys, dvalues)


def pack_owned(grads, owners):
    return jnp.concatenate([g.reshape(owners, -1) for g in grads], axis=1)


def unpack_owned(packed, grads, owners):
    row = packed.reshape(-1)
    pieces = []
    offset = 0
    for g in grads:
        share = g.size // owners
        shard_shape = (g.shape[0] // owners,) + g.shape[1:]
        pieces.append(row[offset : offset + share].reshape(shard_shape))
        offset = offset + share
    return tuple(pieces)


def gather_attention(gain_one, self_proj, self_out, gain_two, cross_query, cross_keyval, cross_out):
    return (
        lax.all_gather(gain_one, ("dp", "fsdp"), axis=0, tiled=True),
        lax.all_gather(self_proj, ("dp", "fsdp"), axis=0, tiled=True),
        lax.all_gather(self_out, ("dp", "fsdp"), axis=0, tiled=True),
        lax.all_gather(gain_two, ("dp", "fsdp"), axis=0, tiled=True),
        lax.all_gather(cross_query, ("dp", "fsdp"), axis=0, tiled=True),
        lax.all_gather(cross_keyval, ("dp", "fsdp"), axis=0, tiled=True),
        lax.all_gather(cross_out, ("dp", "fsdp"), axis=0, tiled=True),
    )


def gather_feed(gain_three, feed_in, feed_bias, feed_down, down_bias):
    return (
        lax.all_gather(gain_three, ("dp", "fsdp"), axis=0, tiled=True),
        lax.all_gather(feed_in, ("dp", "fsdp"), axis=0, tiled=True),
        lax.all_gather(feed_bias, ("dp", "fsdp"), axis=0, tiled=True),
        lax.all_gather(feed_down, ("dp", "fsdp"), axis=0, tiled=True),
        lax.all_gather(down_bias, ("dp", "fsdp"), axis=0, tiled=True),
    )


def sum_attention(grads):
    owners = lax.axis_size("dp") * lax.axis_size("fsdp")
    packed = pack_owned(grads, owners)
    summed = lax.psum_scatter(packed, ("dp", "fsdp"), scatter_dimension=0, tiled=True)
    return unpack_owned(summed, grads, owners)


def sum_feed(grads):
    owners = lax.axis_size("dp") * lax.axis_size("fsdp")
    packed = pack_owned(grads, owners)
    summed = lax.psum_scatter(packed, ("dp", "fsdp"), scatter_dimension=0, tiled=True)
    return unpack_owned(summed, grads, owners)


def per_device(
    tokens,
    lengths,
    positions,
    conditioning,
    gain_one,
    self_proj,
    self_out,
    gain_two,
    cross_query,
    cross_keyval,
    cross_out,
    gain_three,
    feed_in,
    feed_bias,
    feed_down,
    down_bias,
    cotangent,
):
    rows, width = tokens.shape
    cond_rows = conditioning.shape[0]
    bf = jnp.bfloat16
    fl = jnp.float32
    live = jnp.arange(rows, dtype=jnp.int32) < lengths[0]
    key_mask = live[None, None, :]
    quarter = HD // 4
    freq = 10000.0 ** (-jnp.arange(quarter, dtype=fl) / quarter)
    angle = positions.astype(fl)[:, None] * freq[None, :]
    cosine = jnp.cos(angle)[:, None, :]
    sine = jnp.sin(angle)[:, None, :]
    attention_set = gather_attention(
        gain_one, self_proj, self_out, gain_two, cross_query, cross_keyval, cross_out
    )
    g_one, w_proj, w_out, g_two, w_query, w_keyval, w_cross = attention_set
    x_start = tokens.astype(fl)
    h_one, unit_one, rstd_one = norm_rows(x_start, g_one.astype(fl))
    h_one = h_one.astype(bf)
    mixed = jnp.dot(h_one, w_proj, preferred_element_type=fl)
    query = rotate(mixed[:, :width].reshape(rows, HEADS, HD), cosine, sine).astype(bf)
    keys = rotate(mixed[:, width : 2 * width].reshape(rows, HEADS, HD), cosine, sine).astype(bf)
    values = mixed[:, 2 * width :].reshape(rows, HEADS, HD).astype(bf)
    attended, lse_one = attend(query, keys, values, key_mask)
    attended = attended.reshape(rows, width).astype(bf)
    x_one = x_start + jnp.dot(attended, w_out, preferred_element_type=fl)
    h_two, unit_two, rstd_two = norm_rows(x_one, g_two.astype(fl))
    h_two = h_two.astype(bf)
    query_two = (
        jnp.dot(h_two, w_query, preferred_element_type=fl).astype(bf).reshape(rows, HEADS, HD)
    )
    keyval = jnp.dot(conditioning, w_keyval, preferred_element_type=fl).astype(bf)
    keys_two = keyval[:, :width].reshape(cond_rows, HEADS, HD)
    values_two = keyval[:, width:].reshape(cond_rows, HEADS, HD)
    attended_two, lse_two = attend(query_two, keys_two, values_two, None)
    attended_two = attended_two.reshape(rows, width).astype(bf)
    x_two = x_one + jnp.dot(attended_two, w_cross, preferred_element_type=fl)
    feed_set = gather_feed(gain_three, feed_in, feed_bias, feed_down, down_bias)
    g_three, w_in, b_in, w_down, b_down = feed_set
    hidden = w_in.shape[1] // 2
    h_three, unit_three, rstd_three = norm_rows(x_two, g_three.astype(fl))
    h_three = h_three.astype(bf)
    z_pre = jnp.dot(h_three, w_in, preferred_element_type=fl) + b_in.astype(fl)
    value = z_pre[:, :hidden]
    gate = z_pre[:, hidden:]
    sig = jax.nn.sigmoid(gate)
    middle = (value * gate * sig).astype(bf)
    result = x_two + jnp.dot(middle, w_down, preferred_element_type=fl) + b_down.astype(fl)
    output = result.astype(bf)
    feed_set = gather_feed(gain_three, feed_in, feed_bias, feed_down, down_bias)
    g_three, w_in, b_in, w_down, b_down = feed_set
    grad = jnp.where(live[:, None], cotangent.astype(fl), 0.0)
    grad_low = grad.astype(bf)
    down_grad = outer_sum(middle, grad_low)
    dbias_grad = jnp.sum(grad_low.astype(fl), axis=0)
    dmiddle = back_mul(grad_low, w_down)
    dvalue = dmiddle * gate * sig
    dgate = dmiddle * value * sig * (1.0 + gate * (1.0 - sig))
    dz_low = jnp.concatenate([dvalue, dgate], axis=1).astype(bf)
    in_grad = outer_sum(h_three, dz_low)
    bias_grad = jnp.sum(dz_low.astype(fl), axis=0)
    dh_three = back_mul(dz_low, w_in)
    back_three, three_grad = norm_back(dh_three, g_three.astype(fl), unit_three, rstd_three)
    dx_two = grad + back_three
    feed_sums = sum_feed((three_grad, in_grad, bias_grad, down_grad, dbias_grad))
    attention_set = gather_attention(
        gain_one, self_proj, self_out, gain_two, cross_query, cross_keyval, cross_out
    )
    g_one, w_proj, w_out, g_two, w_query, w_keyval, w_cross = attention_set
    d_two = dx_two.astype(bf)
    cross_grad = outer_sum(attended_two, d_two)
    da_two = back_mul(d_two, w_cross).astype(bf).reshape(rows, HEADS, HD)
    dq_two, dk_two, dv_two = attend_back(query_two, keys_two, values_two, None, lse_two, da_two)
    dq_low = dq_two.reshape(rows, width).astype(bf)
    dkeyval = jnp.concatenate(
        [dk_two.reshape(cond_rows, width), dv_two.reshape(cond_rows, width)], axis=1
    ).astype(bf)
    query_grad = outer_sum(h_two, dq_low)
    keyval_grad = outer_sum(conditioning, dkeyval)
    back_two, two_grad = norm_back(back_mul(dq_low, w_query), g_two.astype(fl), unit_two, rstd_two)
    dx_one = dx_two + back_two
    d_one = dx_one.astype(bf)
    out_grad = outer_sum(attended, d_one)
    da_one = back_mul(d_one, w_out).astype(bf).reshape(rows, HEADS, HD)
    dq_one, dk_one, dv_one = attend_back(query, keys, values, key_mask, lse_one, da_one)
    dq_one = rotate(dq_one, cosine, -sine)
    dk_one = rotate(dk_one, cosine, -sine)
    dmixed = jnp.concatenate(
        [dq_one.reshape(rows, width), dk_one.reshape(rows, width), dv_one.reshape(rows, width)],
        axis=1,
    ).astype(bf)
    proj_grad = outer_sum(h_one, dmixed)
    back_one, one_grad = norm_back(back_mul(dmixed, w_proj), g_one.astype(fl), unit_one, rstd_one)
    tokens_grad = dx_one + back_one
    attention_sums = sum_attention(
        (one_grad, proj_grad, out_grad, two_grad, query_grad, keyval_grad, cross_grad)
    )
    return (
        output,
        tokens_grad,
        attention_sums[0],
        attention_sums[1],
        attention_sums[2],
        attention_sums[3],
        attention_sums[4],
        attention_sums[5],
        attention_sums[6],
        feed_sums[0],
        feed_sums[1],
        feed_sums[2],
        feed_sums[3],
        feed_sums[4],
    )


def solution(mesh):
    placed = (
        P(("dp", "fsdp"), None),
        P(("dp", "fsdp")),
        P(("dp", "fsdp")),
        P(("dp", "fsdp"), None),
        P(("dp", "fsdp")),
        P(("dp", "fsdp"), None),
        P(("dp", "fsdp"), None),
        P(("dp", "fsdp")),
        P(("dp", "fsdp"), None),
        P(("dp", "fsdp"), None),
        P(("dp", "fsdp"), None),
        P(("dp", "fsdp")),
        P(("dp", "fsdp"), None),
        P(("dp", "fsdp")),
        P(("dp", "fsdp"), None),
        P(("dp", "fsdp")),
        P(("dp", "fsdp"), None),
    )
    return jax.shard_map(
        per_device,
        mesh=mesh,
        in_specs=placed,
        out_specs=(
            P(("dp", "fsdp"), None),
            P(("dp", "fsdp"), None),
            P(("dp", "fsdp")),
            P(("dp", "fsdp"), None),
            P(("dp", "fsdp"), None),
            P(("dp", "fsdp")),
            P(("dp", "fsdp"), None),
            P(("dp", "fsdp"), None),
            P(("dp", "fsdp"), None),
            P(("dp", "fsdp")),
            P(("dp", "fsdp"), None),
            P(("dp", "fsdp")),
            P(("dp", "fsdp"), None),
            P(("dp", "fsdp")),
        ),
        check_vma=False,
    )
```

profile of v0, /device:TPU:0, one launch (start us, length us, event | category | flops | bytes accessed | tf_op | source)
XLA Modules:
  0.0 3699.2 jit_solution(12738104480633891949)
XLA Ops:
  15.4 42.5 %all-reduce.6 = (bf16[1536]{0:T(1024)(128)(2,1)S(1)}, bf16[1536]{0:T(1024)(128)(2,1)S(1)}, bf16[1536]{0:T(1024)(128)(2,1)S(1)}, bf16[1536]{0:T(1024)(128)(2,1)}) all-reduce(bf16[1536]{0:T(1024)(128)(2,1)S(1)} %dynamic-update-slice, bf16[1536]{0:T(1024)(128)(2,1)S(1)} %dynamic-update-slice.1, ...), channel_id=1, replica_groups=mesh['dp'=4,'fsdp'=8] {'dp','fsdp'}, use_global_device_ids=true, to_apply=%add | all-reduce | flops 6144 | bytes 24576
  60.5 41.3 %all-gather = bf16[32,1,384]{2,1,0:T(2,128)(2,1)S(1)} all-gather(bf16[1,1,384]{2,1,0:T(2,128)(2,1)S(1)} %reshape.362), channel_id=1, replica_groups=mesh['dp'=4,'fsdp'=8] {'dp','fsdp'}, dimensions={0}, use_global_device_ids=true | all-gather | bytes 25344 | tf_op jit(solution)/shard_map/all_gather | solution.py:111
  104.1 3.1 convolution_convert_fusion
  108.4 74.6 %all-gather.9.cloned.1.call-done = bf16[1536,4608]{1,0:T(8,128)(2,1)} async-done(((bf16[48,4608]{1,0:T(8,128)(2,1)}), bf16[1536,4608]{1,0:T(8,128)(2,1)}) %all-gather.9.cloned.1.call-update) | async-done | bytes 14155792 | tf_op jit(solution)/shard_map/all_gather | solution.py:98
  183.1 7.1 fusion.55
  198.4 49.5 %all-gather.11.cloned.1.call-done = bf16[1536,1536]{1,0:T(8,128)(2,1)} async-done(((bf16[48,1536]{1,0:T(8,128)(2,1)}), bf16[1536,1536]{1,0:T(8,128)(2,1)}) %all-gather.11.cloned.1.call-update) | async-done | bytes 4718608 | tf_op jit(solution)/shard_map/all_gather | solution.py:99
  247.9 3.2 fusion.61
  251.5 61.9 %all-gather.15.cloned.1.call-done = bf16[1536,1536]{1,0:T(8,128)(2,1)} async-done(((bf16[48,1536]{1,0:T(8,128)(2,1)}), bf16[1536,1536]{1,0:T(8,128)(2,1)}) %all-gather.15.cloned.1.call-update) | async-done | bytes 4718608 | tf_op jit(solution)/shard_map/all_gather | solution.py:101
  313.3 3.2 convolution_convert_fusion.3
  319.0 59.6 %all-gather.17.cloned.1.call-done = bf16[1536,1536]{1,0:T(8,128)(2,1)} async-done(((bf16[48,1536]{1,0:T(8,128)(2,1)}), bf16[1536,1536]{1,0:T(8,128)(2,1)}) %all-gather.17.cloned.1.call-update) | async-done | bytes 4718608 | tf_op jit(solution)/shard_map/all_gather | solution.py:103
  378.7 3.4 fusion.63
  384.1 211.3 %all-gather.19.cloned.1.call-done = bf16[1536,12288]{1,0:T(8,128)(2,1)} async-done(((bf16[48,12288]{1,0:T(8,128)(2,1)}), bf16[1536,12288]{1,0:T(8,128)(2,1)}) %all-gather.19.cloned.1.call-update) | async-done | bytes 37748752 | tf_op jit(solution)/shard_map/all_gather | solution.py:110
  595.4 17.9 convolution_add_fusion
  613.4 108.0 %all-gather.21.cloned.1.call-done = bf16[6144,1536]{1,0:T(8,128)(2,1)} async-done(((bf16[192,1536]{1,0:T(8,128)(2,1)}), bf16[6144,1536]{1,0:T(8,128)(2,1)}) %all-gather.21.cloned.1.call-update) | async-done | bytes 18874384 | tf_op jit(solution)/shard_map/all_gather | solution.py:112
  721.4 13.1 multiply_convert_fusion.1
  734.5 20.5 multiply_reduce_fusion.2
  758.8 4.7 convolution_convert_fusion.2
  768.6 4.9 multiply_reduce_fusion.3
  784.6 5.1 fusion.35
  789.8 5.1 fusion.57
  796.2 5.1 fusion.38
  802.3 12.9 fusion.33
  815.2 11.3 fusion.23
  826.6 28.6 reshape.334
  855.2 8.1 reshape.335
  863.4 8.1 reshape.337
  871.4 4.9 convolution_bitcast_fusion
  876.4 9.7 copy.90
  886.1 8.1 reshape.340
  894.2 8.2 reshape.341
  903.8 78.7 %dynamic-update-slice.10 = f32[32,516192]{1,0:T(8,128)} dynamic-update-slice(f32[32,516192]{1,0:T(8,128)} %dynamic-update-slice.9, f32[32,221184]{1,0:T(8,128)} %reshape.334, s32[]{} %constant.80, s32[]{} %constant.81) | dynamic-update-slice | bytes 56623108
  982.5 28.8 dynamic-update-slice.11
  1012.7 28.8 dynamic-update-slice.13
  1041.5 28.8 dynamic-update-slice.14
  1070.3 28.3 dynamic-update-slice.15
  1100.1 30.3 fusion.16
  1130.4 69.4 %reshape.348 = f32[32,589824]{1,0:T(8,128)} reshape(f32[1536,12288]{1,0:T(8,128)} %fusion.16) | data formatting | bytes 150994944 | tf_op jit(solution)/shard_map/reshape | solution.py:80
  1201.8 16.5 fusion.50
  1218.3 37.1 %reshape.350 = f32[32,294912]{1,0:T(8,128)} reshape(f32[6144,1536]{1,0:T(8,128)} %fusion.50) | data formatting | bytes 75497472 | tf_op jit(solution)/shard_map/reshape | solution.py:80
  1256.8 206.4 %dynamic-update-slice.5 = f32[32,885216]{1,0:T(8,128)} dynamic-update-slice(f32[32,885216]{1,0:T(8,128)} %dynamic-update-slice.4, f32[32,589824]{1,0:T(8,128)} %reshape.348, s32[]{} %constant.80, s32[]{} %constant.81) | dynamic-update-slice | bytes 150994944
  1464.9 104.1 %dynamic-update-slice.7 = f32[32,885216]{1,0:T(8,128)} dynamic-update-slice(f32[32,885216]{1,0:T(8,128)} %dynamic-update-slice.6, f32[32,294912]{1,0:T(8,128)} %reshape.350, s32[]{} %constant.80, s32[]{} %constant.83) | dynamic-update-slice | bytes 75497472
  1573.1 10.4 fusion.1
  1583.5 471.8 %all-reduce.10.cloned.1.call-done = f32[32,516192]{1,0:T(8,128)} async-done(((f32[32,516192]{1,0:T(8,128)}), f32[32,516192]{1,0:T(8,128)}) %all-reduce.10.cloned.1.call-update) | async-done | bytes 66072592
  2055.3 11.2 dynamic-slice_reduce_fusion.2
  2067.6 8.6 dynamic-slice_reduce_fusion.3
  2080.5 1565.3 %all-reduce.12.cloned.1.call-done = f32[32,885216]{1,0:T(8,128)} async-done(((f32[32,885216]{1,0:T(8,128)}), f32[32,885216]{1,0:T(8,128)}) %all-reduce.12.cloned.1.call-update) | async-done | bytes 113307664
  3645.8 27.0 dynamic-slice_reduce_fusion
  3674.4 14.2 dynamic-slice_reduce_fusion.1
  (289 shorter events, 72.7 us)
Async XLA Ops:
  7.2 96.9 %copy-start = (bf16[128,768]{1,0:T(8,128)(2,1)S(1)}, bf16[128,768]{1,0:T(8,128)(2,1)}, u32[]{:S(2)}) copy-start(bf16[128,768]{1,0:T(8,128)(2,1)} %param.20) | copy-start | bytes 589828
  7.2 95.8 %copy-start.6 = (bf16[128,1536]{1,0:T(8,128)(2,1)S(1)}, bf16[128,1536]{1,0:T(8,128)(2,1)}, u32[]{:S(2)}) copy-start(bf16[128,1536]{1,0:T(8,128)(2,1)} %param.17) | copy-start | bytes 1179652
  7.2 96.9 %all-gather.13.cloned.1.call-start = ((), (), s32[]{:S(2)}) async-start(), calls=%async_computation.2 | async-start | bytes 4866048 | tf_op jit(solution)/shard_map/all_gather | solution.py:102
  7.9 175.1 %all-gather.9.cloned.1.call-start = ((), (), s32[]{:S(2)}) async-start(), calls=%async_computation | async-start | bytes 14598144 | tf_op jit(solution)/shard_map/all_gather | solution.py:98
  8.7 239.2 %all-gather.11.cloned.1.call-start = ((), (), s32[]{:S(2)}) async-start(), calls=%async_computation.1 | async-start | bytes 4866048 | tf_op jit(solution)/shard_map/all_gather | solution.py:99
  9.4 303.9 %all-gather.15.cloned.1.call-start = ((), (), s32[]{:S(2)}) async-start(), calls=%async_computation.3 | async-start | bytes 4866048 | tf_op jit(solution)/shard_map/all_gather | solution.py:101
  10.0 368.7 %all-gather.17.cloned.1.call-start = ((), (), s32[]{:S(2)}) async-start(), calls=%async_computation.4 | async-start | bytes 4866048 | tf_op jit(solution)/shard_map/all_gather | solution.py:103
  10.6 584.8 %all-gather.19.cloned.1.call-start = ((), (), s32[]{:S(2)}) async-start(), calls=%async_computation.5 | async-start | bytes 38928384 | tf_op jit(solution)/shard_map/all_gather | solution.py:110
  11.2 710.2 %all-gather.21.cloned.1.call-start = ((), (), s32[]{:S(2)}) async-start(), calls=%async_computation.6 | async-start | bytes 19464192 | tf_op jit(solution)/shard_map/all_gather | solution.py:112
  11.9 2043.3 %all-reduce.10.cloned.1.call-start = ((), (), s32[]{:S(2)}) async-start(), calls=%async_computation.7 | async-start | bytes 132153344
  57.9 757.4 %copy-start.44 = (f32[1536]{0:T(1024)}, f32[1536]{0:T(1024)S(1)}, u32[]{:S(2)}) copy-start(f32[1536]{0:T(1024)S(1)} %convert_element_type.124) | copy-start | bytes 18436
  103.1 80.0 %copy-start.67 = (f32[128]{0:T(128)}, f32[128]{0:T(128)S(1)}, u32[]{:S(2)}) copy-start(f32[128]{0:T(128)S(1)} %broadcast_multiply_fusion.8) | copy-start | bytes 1540
  103.4 79.7 %copy-start.70 = (f32[128]{0:T(128)}, f32[128]{0:T(128)S(1)}, u32[]{:S(2)}) copy-start(f32[128]{0:T(128)S(1)} %add_rsqrt_fusion.2) | copy-start | bytes 1540
  108.4 208.3 %copy-start.23 = (bf16[128,1536]{0,1:T(8,128)(2,1)}, bf16[128,1536]{0,1:T(8,128)(2,1)S(1)}, u32[]{:S(2)}) copy-start(bf16[128,1536]{0,1:T(8,128)(2,1)S(1)} %copy.80) | copy-start | bytes 1179652
  194.7 2.5 copy-start.34
  194.7 3.3 copy-start.31
  198.4 52.8 %copy-start.28 = (bf16[24,64,128]{2,1,0:T(8,128)(2,1)}, bf16[24,64,128]{2,1,0:T(8,128)(2,1)S(1)}, u32[]{:S(2)}) copy-start(bf16[24,64,128]{2,1,0:T(8,128)(2,1)S(1)} %convolution_convert_fusion.7) | copy-start | bytes 1179652
  247.9 65.4 %copy-start.46 = (f32[1536]{0:T(1024)S(1)}, f32[1536]{0:T(1024)}, u32[]{:S(2)}) copy-start(f32[1536]{0:T(1024)} %convert_element_type.133) | copy-start | bytes 18436
  251.2 65.3 %copy-start.73 = (f32[128]{0:T(128)}, f32[128]{0:T(128)S(1)}, u32[]{:S(2)}) copy-start(f32[128]{0:T(128)S(1)} %broadcast_multiply_fusion.7) | copy-start | bytes 1540
  251.4 65.3 %copy-start.76 = (f32[128]{0:T(128)}, f32[128]{0:T(128)S(1)}, u32[]{:S(2)}) copy-start(f32[128]{0:T(128)S(1)} %add_rsqrt_fusion.1) | copy-start | bytes 1540
  316.7 2.3 copy-start.21
  378.7 4.2 copy-start.53
  378.7 4.2 copy-start.63
  378.7 4.8 copy-start.59
  378.7 4.8 copy-start.61
  382.1 717.3 %copy-start.2 = (f32[128,1536]{1,0:T(8,128)}, f32[128,1536]{1,0:T(8,128)S(1)}, u32[]{:S(2)}) copy-start(f32[128,1536]{1,0:T(8,128)S(1)} %get-tuple-element.66) | copy-start | bytes 2359300
  768.5 5.0 copy-start.26
  768.5 6.2 slice-start
  768.5 5.0 copy-start.13
  768.5 6.2 slice-start.1
  779.1 2.3 copy-start.5
  779.1 4.0 copy-start.51
  784.6 5.1 copy-start.27
  784.6 5.1 copy-start.48
  784.6 5.1 copy-start.75
  784.6 5.1 copy-start.78
  789.7 5.1 copy-start.25
  789.7 5.1 copy-start.50
  789.7 5.8 copy-start.18
  789.7 5.8 copy-start.22
  796.2 5.2 copy-start.54
  796.2 5.2 copy-start.64
  855.2 8.1 copy-start.66
  1098.7 2547.1 %all-reduce.12.cloned.1.call-start = ((), (), s32[]{:S(2)}) async-start(), calls=%async_computation.8 | async-start | bytes 226623488
  1130.4 69.4 %copy-start.20 = (bf16[128,6144]{1,0:T(8,128)(2,1)S(1)}, bf16[128,6144]{1,0:T(8,128)(2,1)}, u32[]{:S(2)}) copy-start(bf16[128,6144]{1,0:T(8,128)(2,1)} %get-tuple-element.35) | copy-start | bytes 4718596
  1218.3 37.1 %copy-start.65 = (f32[1536]{0:T(1024)S(1)}, f32[1536]{0:T(1024)}, u32[]{:S(2)}) copy-start(f32[1536]{0:T(1024)} %get-tuple-element.50) | copy-start | bytes 18436
  1570.5 2.6 copy-start.3
  3672.7 19.7 copy-start.1
  (47 other events, 63.7 us)
Sparse Core Ops, SparseCore 0:
  11.1 66.6 all-gather.12
  80.7 102.3 all-gather.8
  186.1 61.7 all-gather.10
  250.8 62.4 all-gather.14
  316.2 62.4 all-gather.16
  381.6 213.8 all-gather.18
  598.4 122.8 all-gather.20
  1098.8 956.4 all-reduce.9
  2062.8 1582.9 all-reduce.11
where the time goes:
time: 3720 us; the launch traced here: 3700 us
  waiting for transfers between devices  2610 us (70%)
  local copies, waits for them, and re-layouts  782 us (21%)
  matrix products  197 us (5%)
  blocking collectives  83.7 us (2%)
    unnamed x11, waiting for transfers between devices  2040 us
    unnamed x191, local copies, waits for them, and re-layouts  494 us
    all_gather x1, waiting for transfers between devices, gather_feed(): lax.all_gather(feed_in, ('dp', 'fsdp'), axis=0, tiled=True)  211 us
    reshape x12, local copies, waits for them, and re-layouts, pack_owned(): return jnp.concatenate([g.reshape(owners, -1) for g in grads], axis=1)  168 us
    all_gather x1, waiting for transfers between devices, gather_feed(): lax.all_gather(feed_down, ('dp', 'fsdp'), axis=0, tiled=True)  108 us
    dot_general x7, matrix products, outer_sum(): lax.dot_general(left, right, (((0,), (0,)), ((), ())), preferred_element_...  79.9 us
    all_gather x1, waiting for transfers between devices, gather_attention(): lax.all_gather(self_proj, ('dp', 'fsdp'), axis=0, tiled=True)  74.6 us
  transfers between devices with their start and end apart: 9, of which 8 were waited for; matrix products, arithmetic and copies ran while one was open for 15% of the time, Pallas kernels for 0%

commit v1 on v0

v1 whole, which is shorter than its diff:
```python
import jax
import jax.numpy as jnp
from jax import lax
from jax.sharding import PartitionSpec as P

HEADS = 24
HD = 64
BF = jnp.bfloat16
FL = jnp.float32


def xor_perm(k, size):
    return [(i, i ^ k) for i in range(size)]


def across(v, k):
    return lax.ppermute(v, "dp", xor_perm(k, lax.axis_size("dp")))


def swap_core(v):
    return lax.ppermute(v, "fsdp", xor_perm(1, lax.axis_size("fsdp")))


def ring_next(v):
    nf = lax.axis_size("fsdp")
    return lax.ppermute(v, "fsdp", [(i, (i + 2) % nf) for i in range(nf)])


def place(buf, piece, starts):
    return lax.dynamic_update_slice(buf, piece.reshape(piece.shape), starts)


def gather_line(chunk):
    nf = lax.axis_size("fsdp")
    nz = nf // 2
    f = lax.axis_index("fsdp")
    z, c = f // 2, f % 2
    buf = jnp.zeros((nz, 2) + chunk.shape, chunk.dtype)
    v = chunk
    zero = (0,) * chunk.ndim
    for s in range(nz):
        if s:
            v = ring_next(v)
        u = swap_core(v)
        at = (z - s) % nz
        buf = lax.dynamic_update_slice(buf, v[None, None], (at, c) + zero)
        buf = lax.dynamic_update_slice(buf, u[None, None], (at, 1 - c) + zero)
    return buf


def reduce_line(parts):
    nf = lax.axis_size("fsdp")
    nz = nf // 2
    f = lax.axis_index("fsdp")
    z, c = f // 2, f % 2
    give = lax.dynamic_index_in_dim(parts, 1 - c, 1, keepdims=False)
    keep = lax.dynamic_index_in_dim(parts, c, 1, keepdims=False)
    got = swap_core(give)
    summed = (keep.astype(FL) + got.astype(FL)).astype(BF)
    acc = None
    for s in range(1, nz + 1):
        own = lax.dynamic_index_in_dim(summed, (z - s) % nz, 0, keepdims=False)
        acc = own.astype(FL) if acc is None else own.astype(FL) + acc.astype(FL)
        if s < nz:
            acc = ring_next(acc.astype(BF))
    return acc


def gather_dp(v):
    n = lax.axis_size("dp")
    t = lax.axis_index("dp")
    buf = jnp.zeros((n,) + v.shape, v.dtype)
    zero = (0,) * v.ndim
    for k in range(n):
        got = across(v, k) if k else v
        buf = lax.dynamic_update_slice(buf, got[None], (t ^ k,) + zero)
    return buf


def reduce_dp(parts):
    n = lax.axis_size("dp")
    t = lax.axis_index("dp")
    low = parts.astype(BF)
    acc = lax.dynamic_index_in_dim(parts, t, 0, keepdims=False)
    for k in range(1, n):
        got = across(lax.dynamic_index_in_dim(low, t ^ k, 0, keepdims=False), k)
        acc = acc + got.astype(FL)
    return acc


def swap_dp(v):
    n = lax.axis_size("dp")
    t = lax.axis_index("dp")
    buf = jnp.zeros(v.shape, v.dtype)
    zero = (0,) * (v.ndim - 1)
    for k in range(n):
        got = lax.dynamic_slice_in_dim(v, t ^ k, 1, 0)
        if k:
            got = across(got, k)
        buf = lax.dynamic_update_slice(buf, got, (t ^ k,) + zero)
    return buf


def columns_of(weight, sections):
    n = lax.axis_size("dp")
    rows, width = weight.shape
    share = width // sections // n
    cut = lambda s, j: weight[:, s * n * share + j * share : s * n * share + (j + 1) * share]
    return jnp.stack([jnp.concatenate([cut(s, j) for s in range(sections)], axis=1) for j in range(n)])


def columns_back(parts, sections):
    n, rows, width = parts.shape
    share = width // sections
    return jnp.concatenate(
        [parts[j, :, s * share : (s + 1) * share] for s in range(sections) for j in range(n)], axis=1
    )


def gather_columns(weight, sections):
    chunk = swap_dp(columns_of(weight, sections))
    full = gather_line(chunk)
    n, rows, width = chunk.shape
    return full.transpose(2, 0, 1, 3, 4).reshape(-1, width)


def gather_rows(weight):
    return gather_line(weight).reshape(-1, weight.shape[1])


def reduce_columns(grad, sections):
    n = lax.axis_size("dp")
    nf = lax.axis_size("fsdp")
    width = grad.shape[1]
    parts = grad.astype(BF).reshape(n, nf // 2, 2, -1, width).transpose(1, 2, 0, 3, 4)
    mine = reduce_line(parts).astype(BF)
    return columns_back(swap_dp(mine).astype(FL), sections)


def reduce_rows(grad):
    nf = lax.axis_size("fsdp")
    return reduce_line(grad.astype(BF).reshape(nf // 2, 2, -1, grad.shape[1]))


def norm_rows(v, gain):
    centre = v - jnp.mean(v, axis=-1, keepdims=True)
    rstd = lax.rsqrt(jnp.mean(centre * centre, axis=-1, keepdims=True) + 1e-05)
    unit = centre * rstd
    return unit * gain, unit, rstd


def norm_back(grad, gain, unit, rstd):
    scaled = grad * gain
    return rstd * (
        scaled
        - jnp.mean(scaled, axis=-1, keepdims=True)
        - unit * jnp.mean(scaled * unit, axis=-1, keepdims=True)
    )


def outer_sum(left, right):
    return lax.dot_general(left, right, (((0,), (0,)), ((), ())), preferred_element_type=FL)


def back_mul(grad, weight):
    return lax.dot_general(grad, weight, (((1,), (1,)), ((), ())), preferred_element_type=FL)


def mul(a, b):
    return jnp.dot(a, b, preferred_element_type=FL)


def rotate(t, cosine, sine):
    quarter = cosine.shape[-1]
    first = t[..., :quarter]
    second = t[..., quarter : 2 * quarter]
    return jnp.concatenate(
        [first * cosine - second * sine, second * cosine + first * sine, t[..., 2 * quarter :]], axis=-1
    )


def raw_scores(query, keys, mask):
    scores = jnp.einsum("gqhd,gkhd->ghqk", query, keys, preferred_element_type=FL) * 0.125
    if mask is not None:
        scores = jnp.where(mask, scores, -1e30)
    return scores


def attend(query, keys, values, mask):
    scores = raw_scores(query, keys, mask)
    top = jnp.max(scores, axis=-1, keepdims=True)
    weight = jnp.exp(scores - top)
    total = jnp.sum(weight, axis=-1, keepdims=True)
    probs = (weight / total).astype(BF)
    result = jnp.einsum("ghqk,gkhd->gqhd", probs, values, preferred_element_type=FL)
    return result, top + jnp.log(total)


def attend_back(query, keys, values, mask, lse, grad_out):
    probs = jnp.exp(raw_scores(query, keys, mask) - lse)
    dprob = jnp.einsum("gqhd,gkhd->ghqk", grad_out, values, preferred_element_type=FL)
    dvalues = jnp.einsum("ghqk,gqhd->gkhd", probs.astype(BF), grad_out, preferred_element_type=FL)
    delta = jnp.sum(dprob * probs, axis=-1, keepdims=True)
    dscore = (probs * (dprob - delta)).astype(BF)
    dquery = jnp.einsum("ghqk,gkhd->gqhd", dscore, keys, preferred_element_type=FL) * 0.125
    dkeys = jnp.einsum("ghqk,gqhd->gkhd", dscore, query, preferred_element_type=FL) * 0.125
    return dquery, dkeys, dvalues


def per_device(
    tokens,
    lengths,
    positions,
    conditioning,
    gain_one,
    self_proj,
    self_out,
    gain_two,
    cross_query,
    cross_keyval,
    cross_out,
    gain_three,
    feed_in,
    feed_bias,
    feed_down,
    down_bias,
    cotangent,
):
    rows, width = tokens.shape
    n, nf = lax.axis_size("dp"), lax.axis_size("fsdp")
    t, f = lax.axis_index("dp"), lax.axis_index("fsdp")
    crows, cwidth = conditioning.shape
    heads = HEADS // n
    hw = heads * HD
    owner = lambda a, b: (b // (nf // 2)) * (n * nf // 2) + a * (nf // 2) + b % (nf // 2)
    to_rank = [(owner(a, b), a * nf + b) for a in range(n) for b in range(nf)]
    to_owner = [(b, a) for a, b in to_rank]

    small = gather_dp(jnp.concatenate([gain_one, gain_two, gain_three, down_bias]))
    bias_piece = lax.ppermute(feed_bias, ("dp", "fsdp"), to_rank)
    every = gather_line(jnp.concatenate([small.reshape(-1), bias_piece]))
    share = gain_one.shape[0]
    vectors = every[:, :, : n * 4 * share].reshape(nf, n, 4, share).transpose(2, 1, 0, 3).reshape(4, width)
    g_one, g_two, g_three, b_down = vectors.astype(FL)
    b_in = every[:, :, n * 4 * share :].reshape(-1).astype(FL)

    info = gather_dp(jnp.concatenate([positions, jnp.broadcast_to(lengths, (rows,))]).reshape(2, rows))
    places = info[:, 0]
    live_all = jnp.arange(rows, dtype=jnp.int32)[None, :] < info[:, 1]
    key_mask = live_all[:, None, None, :]
    quarter = HD // 4
    freq = 10000.0 ** (-jnp.arange(quarter, dtype=FL) / quarter)
    angle = places.astype(FL)[:, :, None] * freq
    cosine = jnp.cos(angle)[:, :, None, :]
    sine = jnp.sin(angle)[:, :, None, :]

    w_proj = gather_columns(self_proj, 3)
    w_out = gather_rows(self_out)
    w_query = gather_columns(cross_query, 1)
    w_keyval = gather_columns(cross_keyval, 2)
    w_cross = gather_rows(cross_out)
    w_in = gather_columns(feed_in, 2)
    w_down = gather_rows(feed_down)

    live = jnp.arange(rows, dtype=jnp.int32) < lengths[0]
    grad = jnp.where(live[:, None], cotangent.astype(FL), 0.0)
    grad_all = gather_dp(grad.astype(BF)).reshape(n * rows, width)
    cond_all = gather_dp(conditioning).reshape(n * crows, cwidth)

    x_start = tokens.astype(FL)
    h_one, unit_one, rstd_one = norm_rows(x_start, g_one)
    h_one = gather_dp(h_one.astype(BF)).reshape(n * rows, width)
    mixed = mul(h_one, w_proj).reshape(n, rows, 3, heads, HD)
    query = rotate(mixed[:, :, 0], cosine, sine).astype(BF)
    keys = rotate(mixed[:, :, 1], cosine, sine).astype(BF)
    values = mixed[:, :, 2].astype(BF)
    attended, lse_one = attend(query, keys, values, key_mask)
    attended = attended.reshape(n * rows, hw).astype(BF)
    x_one = x_start + reduce_dp(mul(attended, w_out).reshape(n, rows, width))

    h_two, unit_two, rstd_two = norm_rows(x_one, g_two)
    h_two = gather_dp(h_two.astype(BF)).reshape(n * rows, width)
    query_two = mul(h_two, w_query).astype(BF).reshape(n, rows, heads, HD)
    keyval = mul(cond_all, w_keyval).astype(BF).reshape(n, crows, 2, heads, HD)
    keys_two, values_two = keyval[:, :, 0], keyval[:, :, 1]
    attended_two, lse_two = attend(query_two, keys_two, values_two, None)
    attended_two = attended_two.reshape(n * rows, hw).astype(BF)
    x_two = x_one + reduce_dp(mul(attended_two, w_cross).reshape(n, rows, width))

    h_three, unit_three, rstd_three = norm_rows(x_two, g_three)
    h_three = gather_dp(h_three.astype(BF)).reshape(n * rows, width)
    hidden = w_in.shape[1] // 2
    z_pre = mul(h_three, w_in) + b_in
    value, gate = z_pre[:, :hidden], z_pre[:, hidden:]
    sig = jax.nn.sigmoid(gate)
    middle = (value * gate * sig).astype(BF)
    result = x_two + reduce_dp(mul(middle, w_down).reshape(n, rows, width)) + b_down
    output = result.astype(BF)
    down_grad = reduce_rows(outer_sum(middle, grad_all))
    dmiddle = back_mul(grad_all, w_down)
    dvalue = dmiddle * gate * sig
    dgate = dmiddle * value * sig * (1.0 + gate * (1.0 - sig))
    dz = jnp.concatenate([dvalue, dgate], axis=1).astype(BF)
    in_grad = reduce_columns(outer_sum(h_three, dz), 2)
    dh_three = reduce_dp(back_mul(dz, w_in).reshape(n, rows, width))
    dx_two = grad + norm_back(dh_three, g_three, unit_three, rstd_three)

    down_cols = jnp.sum(grad_all.astype(FL), axis=0).reshape(n, nf, share)
    down_cols = lax.dynamic_index_in_dim(down_cols, t, 0, keepdims=False)
    in_cols = jnp.sum(dz.astype(FL), axis=0).reshape(nf, -1)
    cols = jnp.concatenate([in_cols, down_cols], axis=1).reshape(nf // 2, 2, -1)
    cols = reduce_line(cols.astype(BF))
    dbias_grad = cols[in_cols.shape[1] :]
    bias_grad = lax.ppermute(cols[: in_cols.shape[1]], ("dp", "fsdp"), to_owner)

    d_two = gather_dp(dx_two.astype(BF)).reshape(n * rows, width)
    cross_grad = reduce_rows(outer_sum(attended_two, d_two))
    da_two = back_mul(d_two, w_cross).astype(BF).reshape(n, rows, heads, HD)
    dq_two, dk_two, dv_two = attend_back(query_two, keys_two, values_two, None, lse_two, da_two)
    dq_low = dq_two.reshape(n * rows, hw).astype(BF)
    dkeyval = jnp.concatenate(
        [dk_two.reshape(n * crows, hw), dv_two.reshape(n * crows, hw)], axis=1
    ).astype(BF)
    query_grad = reduce_columns(outer_sum(h_two, dq_low), 1)
    keyval_grad = reduce_columns(outer_sum(cond_all, dkeyval), 2)
    dh_two = reduce_dp(back_mul(dq_low, w_query).reshape(n, rows, width))
    dx_one = dx_two + norm_back(dh_two, g_two, unit_two, rstd_two)

    d_one = gather_dp(dx_one.astype(BF)).reshape(n * rows, width)
    out_grad = reduce_rows(outer_sum(attended, d_one))
    da_one = back_mul(d_one, w_out).astype(BF).reshape(n, rows, heads, HD)
    dq_one, dk_one, dv_one = attend_back(query, keys, values, key_mask, lse_one, da_one)
    dq_one = rotate(dq_one, cosine, -sine)
    dk_one = rotate(dk_one, cosine, -sine)
    dmixed = jnp.concatenate(
        [v.reshape(n * rows, hw) for v in (dq_one, dk_one, dv_one)], axis=1
    ).astype(BF)
    proj_grad = reduce_columns(outer_sum(h_one, dmixed), 3)
    dh_one = reduce_dp(back_mul(dmixed, w_proj).reshape(n, rows, width))
    tokens_grad = dx_one + norm_back(dh_one, g_one, unit_one, rstd_one)

    def gain_grad(weight, weight_grad, gain):
        return jnp.sum(weight.astype(FL) * weight_grad, axis=1) / gain.astype(FL)

    return (
        output,
        tokens_grad,
        gain_grad(self_proj, proj_grad, gain_one),
        proj_grad,
        out_grad,
        gain_grad(cross_query, query_grad, gain_two),
        query_grad,
        keyval_grad,
        cross_grad,
        gain_grad(feed_in, in_grad, gain_three),
        in_grad,
        bias_grad,
        down_grad,
        dbias_grad,
    )


def solution(mesh):
    both = ("dp", "fsdp")
    row, flat = P(both, None), P(both)
    return jax.shard_map(
        per_device,
        mesh=mesh,
        in_specs=(row, flat, flat, row, flat, row, row, flat, row, row, row, flat, row, flat, row, flat, row),
        out_specs=(row, row, flat, row, row, flat, row, row, row, flat, row, flat, row, flat),
        check_vma=False,
    )
```

time: 3720 us -> 933 us (0.25)
  waiting for transfers between devices: 2610 us -> 485 us
  local copies, waits for them, and re-layouts: 782 us -> 182 us
  starting transfers between devices: 0.35 us -> 125 us
  matrix products: 197 us -> 81.3 us
  blocking collectives: 83.7 us -> 0 us
    unnamed x11 -> x0, waiting for transfers between devices: 2040 us -> none
    all_gather x7 -> x0, waiting for transfers between devices: 565 us -> none  [the longest x1 211 us: gather_feed(): lax.all_gather(feed_in, ('dp', 'fsdp'), axis=0, tiled=True)]
    ppermute x0 -> x159, waiting for transfers between devices: none -> 485 us  [the longest x48 314 us: ring_next(): return lax.ppermute(v, 'fsdp', [(i, (i + 2) % nf) for i in range(nf)])]
    unnamed x191 -> x271, local copies, waits for them, and re-layouts: 494 us -> 25 us
    reshape x19 -> x7, local copies, waits for them, and re-layouts: 175 us -> 3.56 us  [the longest x1 2.44 us: per_device(): keyval = mul(cond_all, w_keyval).astype(BF).reshape(n, crows, 2, heads, HD)]
    ppermute x0 -> x159, starting transfers between devices: none -> 125 us  [the longest x69 101 us: across(): return lax.ppermute(v, 'dp', xor_perm(k, lax.axis_size('dp')))]
    dynamic_update_slice x0 -> x119, local copies, waits for them, and re-layouts: none -> 94.4 us  [the longest x34 47.3 us: gather_line(): buf = lax.dynamic_update_slice(buf, v[None, None], (at, c) + zero)]
    slice x15 -> x5, local copies, waits for them, and re-layouts: 69.1 us -> 3.97 us  [the longest x1 2.32 us: per_device(): keys_two, values_two = (keyval[:, :, 0], keyval[:, :, 1])]
  transfers between devices with their start and end apart: 9 -> 159, of which waited for: 8 -> 77; matrix products, arithmetic and copies ran while one was open for 15% -> 27% of each run, Pallas kernels for 0% -> 0%
where the time goes in v1:
time: 933 us; the launch traced here: 922 us
  waiting for transfers between devices  485 us (52%)
  local copies, waits for them, and re-layouts  182 us (20%)
  starting transfers between devices  125 us (13%)
  matrix products  81.3 us (9%)
  other arithmetic  44.1 us (5%)
    ppermute x48, waiting for transfers between devices, ring_next(): return lax.ppermute(v, 'fsdp', [(i, (i + 2) % nf) for i in range(nf)])  314 us
    ppermute x69, waiting for transfers between devices, across(): return lax.ppermute(v, 'dp', xor_perm(k, lax.axis_size('dp')))  167 us
    ppermute x69, starting transfers between devices, across(): return lax.ppermute(v, 'dp', xor_perm(k, lax.axis_size('dp')))  101 us
    dynamic_update_slice x34, local copies, waits for them, and re-layouts, gather_line(): buf = lax.dynamic_update_slice(buf, v[None, None], (at, c) + zero)  47.3 us
    dot_general x7, matrix products, mul(): return jnp.dot(a, b, preferred_element_type=FL)  28.5 us
    dynamic_update_slice x31, local copies, waits for them, and re-layouts, gather_line(): buf = lax.dynamic_update_slice(buf, u[None, None], (at, 1 - c) + zero)  28.4 us
    unnamed x271, local copies, waits for them, and re-layouts  25 us
    dot_general x6, matrix products, back_mul(): lax.dot_general(grad, weight, (((1,), (1,)), ((), ())), preferred_element...  23.6 us
  transfers between devices with their start and end apart: 159, of which 77 were waited for; matrix products, arithmetic and copies ran while one was open for 27% of the time, Pallas kernels for 0%

profile of v1, /device:TPU:0, one launch (start us, length us, event | category | flops | bytes accessed | tf_op | source)
XLA Modules:
  0.0 921.8 jit_solution(7128164144017325964)
XLA Ops:
  115.4 7.1 collective-permute-done.44
  124.6 6.9 collective-permute-done.57
  137.8 12.5 %collective-permute-done.76 = bf16[1,48,3072]{2,1,0:T(8,128)(2,1)S(1)} collective-permute-done((bf16[1,48,3072]{2,1,0:T(8,128)(2,1)S(1)}, bf16[1,48,3072]{2,1,0:T(8,128)(2,1)S(1)}, u32[]{:S(2)}, u32[]{:S(2)}) %collective-permute-start.76) | collective-permute-done | bytes 294944 | tf_op jit(solution)/shard_map/ppermute | solution.py:17
  173.9 7.6 collective-permute-done.66
  183.8 7.2 collective-permute-done.30
  193.1 7.0 collective-permute-done.46
  202.1 7.0 collective-permute-done.59
  224.1 6.9 collective-permute-done.12
  235.8 8.8 collective-permute-done.68
  246.7 7.0 collective-permute-done.32
  255.8 7.1 collective-permute-done.61
  267.6 7.4 collective-permute-done.48
  296.0 20.0 %collective-permute-done.20 = bf16[4,48,1152]{2,1,0:T(8,128)(2,1)} collective-permute-done((bf16[4,48,1152]{2,1,0:T(8,128)(2,1)}, bf16[4,48,1152]{2,1,0:T(8,128)(2,1)}, u32[]{:S(2)}, u32[]{:S(2)}) %collective-permute-start.20) | collective-permute-done | bytes 442400 | tf_op jit(solution)/shard_map/ppermute | solution.py:26
  318.2 10.4 %collective-permute-done.89 = bf16[192,1536]{1,0:T(8,128)(2,1)} collective-permute-done((bf16[192,1536]{1,0:T(8,128)(2,1)}, bf16[192,1536]{1,0:T(8,128)(2,1)}, u32[]{:S(2)}, u32[]{:S(2)}) %collective-permute-start.89) | collective-permute-done | bytes 589856 | tf_op jit(solution)/shard_map/ppermute | solution.py:26
  331.5 6.5 collective-permute-done.22
  364.7 6.4 collective-permute-done.36
  371.2 7.6 collective-permute-done.35
  384.6 7.6 collective-permute-done.50
  392.1 9.1 collective-permute-start.84
  414.3 7.0 collective-permute-done.72
  421.3 5.5 collective-permute-done.71
  442.4 11.1 %collective-permute-done.74 = bf16[128,1536]{1,0:T(8,128)(2,1)S(1)} collective-permute-done((bf16[128,1536]{1,0:T(8,128)(2,1)S(1)}, bf16[128,1536]{1,0:T(8,128)(2,1)S(1)}, u32[]{:S(2)}, u32[]{:S(2)}) %collective-permute-start.74) | collective-permute-done | bytes 393248 | tf_op jit(solution)/shard_map/ppermute | solution.py:17
  459.9 8.7 copy.174
  470.9 8.1 convolution_add_fusion
  479.0 7.7 multiply_convert_fusion.1
  486.8 9.5 %convolution_convert_fusion = bf16[1536,3072]{1,0:T(8,128)(2,1)} fusion(bf16[512,1536]{1,0:T(8,128)(2,1)} %bitcast.128, bf16[512,1536]{1,0:T(8,128)(2,1)S(1)} %get-tuple-element.46, bf16[512,1536]{1,0:T(8,128)(2,1)S(1)} %get-tuple-element.45), kind=kOutput, calls=%fused_computation | convolution fusion | flops 4842848256 | bytes 14155776 | tf_op jit(solution)/shard_map/dot_general | solution.py:162
  497.5 6.7 fusion.168
  510.9 7.2 fusion.169
  523.8 7.1 constant_dynamic-slice_fusion.12
  553.7 6.4 collective-permute-start.103
  563.5 13.5 %collective-permute-done.103 = bf16[128,1536]{1,0:T(8,128)(2,1)S(1)} collective-permute-done((bf16[128,1536]{1,0:T(8,128)(2,1)S(1)}, bf16[128,1536]{1,0:T(8,128)(2,1)S(1)}, u32[]{:S(2)}, u32[]{:S(2)}) %collective-permute-start.103) | collective-permute-done | bytes 393248 | tf_op jit(solution)/shard_map/ppermute | solution.py:17
  599.4 5.9 collective-permute-done.106
  613.2 7.2 collective-permute-done.126
  621.1 6.2 collective-permute-done.133
  628.1 6.2 collective-permute-done.140
  636.2 6.8 collective-permute-done.110
  678.9 7.2 collective-permute-done.128
  686.1 7.9 collective-permute-done.135
  694.4 6.8 collective-permute-done.142
  745.8 5.7 collective-permute-done.123
  752.3 11.9 %collective-permute-done.156 = bf16[192,1536]{1,0:T(8,128)(2,1)S(1)} collective-permute-done((bf16[192,1536]{1,0:T(8,128)(2,1)S(1)}, bf16[192,1536]{1,0:T(8,128)(2,1)S(1)}, u32[]{:S(2)}, u32[]{:S(2)}) %collective-permute-start.156) | collective-permute-done | bytes 589856 | tf_op jit(solution)/shard_map/ppermute | solution.py:26
  764.4 12.4 %collective-permute-done.115 = bf16[4,48,1152]{2,1,0:T(8,128)(2,1)S(1)} collective-permute-done((bf16[4,48,1152]{2,1,0:T(8,128)(2,1)S(1)}, bf16[4,48,1152]{2,1,0:T(8,128)(2,1)S(1)}, u32[]{:S(2)}, u32[]{:S(2)}) %collective-permute-start.115) | collective-permute-done | bytes 442400 | tf_op jit(solution)/shard_map/ppermute | solution.py:26
  777.7 19.9 %collective-permute-done.116 = bf16[4,48,1152]{2,1,0:T(8,128)(2,1)S(1)} collective-permute-done((bf16[4,48,1152]{2,1,0:T(8,128)(2,1)S(1)}, bf16[4,48,1152]{2,1,0:T(8,128)(2,1)S(1)}, u32[]{:S(2)}, u32[]{:S(2)}) %collective-permute-start.116) | collective-permute-done | bytes 442400 | tf_op jit(solution)/shard_map/ppermute | solution.py:26
  798.0 14.7 %collective-permute-done.117 = bf16[4,48,1152]{2,1,0:T(8,128)(2,1)S(1)} collective-permute-done((bf16[4,48,1152]{2,1,0:T(8,128)(2,1)S(1)}, bf16[4,48,1152]{2,1,0:T(8,128)(2,1)S(1)}, u32[]{:S(2)}, u32[]{:S(2)}) %collective-permute-start.117) | collective-permute-done | bytes 442400 | tf_op jit(solution)/shard_map/ppermute | solution.py:26
  817.5 7.8 collective-permute-done.158
  832.6 15.9 %collective-permute-done.144 = bf16[4,48,3072]{2,1,0:T(8,128)(2,1)S(1)} collective-permute-done((bf16[4,48,3072]{2,1,0:T(8,128)(2,1)S(1)}, bf16[4,48,3072]{2,1,0:T(8,128)(2,1)S(1)}, u32[]{:S(2)}, u32[]{:S(2)}) %collective-permute-start.144) | collective-permute-done | bytes 1179680 | tf_op jit(solution)/shard_map/ppermute | solution.py:26
  849.0 27.5 %collective-permute-done.145 = bf16[4,48,3072]{2,1,0:T(8,128)(2,1)S(1)} collective-permute-done((bf16[4,48,3072]{2,1,0:T(8,128)(2,1)S(1)}, bf16[4,48,3072]{2,1,0:T(8,128)(2,1)S(1)}, u32[]{:S(2)}, u32[]{:S(2)}) %collective-permute-start.145) | collective-permute-done | bytes 1179680 | tf_op jit(solution)/shard_map/ppermute | solution.py:26
  877.1 26.5 %collective-permute-done.146 = bf16[4,48,3072]{2,1,0:T(8,128)(2,1)S(1)} collective-permute-done((bf16[4,48,3072]{2,1,0:T(8,128)(2,1)S(1)}, bf16[4,48,3072]{2,1,0:T(8,128)(2,1)S(1)}, u32[]{:S(2)}, u32[]{:S(2)}) %collective-permute-start.146) | collective-permute-done | bytes 1179680 | tf_op jit(solution)/shard_map/ppermute | solution.py:26
  (915 shorter events, 461.6 us)
Async XLA Ops:
  1.6 33.1 %collective-permute-start = (bf16[192]{0:T(256)(128)(2,1)S(1)}, bf16[192]{0:T(256)(128)(2,1)S(1)}, u32[]{:S(2)}, u32[]{:S(2)}) collective-permute-start(bf16[192]{0:T(256)(128)(2,1)S(1)} %pad_maximum_fusion.13), channel_id=1, source_target_pairs={{0,8},{8,0},{16,24},{24,16},{1,9},{9,1},{17,25},{25,17},{2,10},{10... | collective-permute-start | bytes 1160 | tf_op jit(solution)/shard_map/ppermute | solution.py:17
  4.5 32.8 %collective-permute-start.1 = (bf16[192]{0:T(256)(128)(2,1)S(1)}, bf16[192]{0:T(256)(128)(2,1)S(1)}, u32[]{:S(2)}, u32[]{:S(2)}) collective-permute-start(bf16[192]{0:T(256)(128)(2,1)S(1)} %pad_maximum_fusion.13), channel_id=1, source_target_pairs={{0,16},{8,24},{16,0},{24,8},{1,17},{9,25},{17,1},{25,9},{2,18},{10... | collective-permute-start | bytes 1160 | tf_op jit(solution)/shard_map/ppermute | solution.py:17
  6.1 31.5 %collective-permute-start.2 = (bf16[192]{0:T(256)(128)(2,1)S(1)}, bf16[192]{0:T(256)(128)(2,1)S(1)}, u32[]{:S(2)}, u32[]{:S(2)}) collective-permute-start(bf16[192]{0:T(256)(128)(2,1)S(1)} %pad_maximum_fusion.13), channel_id=1, source_target_pairs={{0,24},{8,16},{16,8},{24,0},{1,25},{9,17},{17,9},{25,1},{2,26},{10... | collective-permute-start | bytes 1160 | tf_op jit(solution)/shard_map/ppermute | solution.py:17
  6.1 31.8 %collective-permute-start.3 = (bf16[384]{0:T(512)(128)(2,1)}, bf16[384]{0:T(512)(128)(2,1)S(1)}, u32[]{:S(2)}, u32[]{:S(2)}) collective-permute-start(bf16[384]{0:T(512)(128)(2,1)} %param.30), channel_id=1, source_target_pairs={{0,0},{1,1},{2,2},{3,3},{16,4},{17,5},{18,6},{19,7},{4,8},{5,9},{6... | collective-permute-start | bytes 2312 | tf_op jit(solution)/shard_map/ppermute | solution.py:240
  8.7 31.1 %collective-permute-start.24 = (s32[2,128]{1,0:T(2,128)S(1)}, s32[2,128]{1,0:T(2,128)S(1)}, u32[]{:S(2)}, u32[]{:S(2)}) collective-permute-start(s32[2,128]{1,0:T(2,128)S(1)} %get-tuple-element.170), channel_id=1, source_target_pairs={{0,8},{8,0},{16,24},{24,16},{1,9},{9,1},{17,25},{25,17},{2,10},{10... | collective-permute-start | bytes 3080 | tf_op jit(solution)/shard_map/ppermute | solution.py:17
  37.5 65.7 %collective-permute-start.63 = (bf16[48,1536]{1,0:T(8,128)(2,1)}, bf16[48,1536]{1,0:T(8,128)(2,1)}, u32[]{:S(2)}, u32[]{:S(2)}) collective-permute-start(bf16[48,1536]{1,0:T(8,128)(2,1)} %param.27), channel_id=1, source_target_pairs={{0,1},{1,0},{2,3},{3,2},{4,5},{5,4},{6,7},{7,6},{8,9},{9,8},{10,11... | collective-permute-start | bytes 442376 | tf_op jit(solution)/shard_map/ppermute | solution.py:21
  54.4 52.4 %collective-permute-start.64 = (bf16[48,1536]{1,0:T(8,128)(2,1)}, bf16[48,1536]{1,0:T(8,128)(2,1)}, u32[]{:S(2)}, u32[]{:S(2)}) collective-permute-start(bf16[48,1536]{1,0:T(8,128)(2,1)} %param.27), channel_id=1, source_target_pairs={{0,2},{1,3},{2,4},{3,5},{4,6},{5,7},{6,0},{7,1},{8,10},{9,11},{10,... | collective-permute-start | bytes 442376 | tf_op jit(solution)/shard_map/ppermute | solution.py:26
  54.6 55.3 %collective-permute-start.27 = (bf16[48,1536]{1,0:T(8,128)(2,1)}, bf16[48,1536]{1,0:T(8,128)(2,1)}, u32[]{:S(2)}, u32[]{:S(2)}) collective-permute-start(bf16[48,1536]{1,0:T(8,128)(2,1)} %param.23), channel_id=1, source_target_pairs={{0,1},{1,0},{2,3},{3,2},{4,5},{5,4},{6,7},{7,6},{8,9},{9,8},{10,11... | collective-permute-start | bytes 442376 | tf_op jit(solution)/shard_map/ppermute | solution.py:21
  55.3 56.7 %collective-permute-start.28 = (bf16[48,1536]{1,0:T(8,128)(2,1)}, bf16[48,1536]{1,0:T(8,128)(2,1)}, u32[]{:S(2)}, u32[]{:S(2)}) collective-permute-start(bf16[48,1536]{1,0:T(8,128)(2,1)} %param.23), channel_id=1, source_target_pairs={{0,2},{1,3},{2,4},{3,5},{4,6},{5,7},{6,0},{7,1},{8,10},{9,11},{10,... | collective-permute-start | bytes 442376 | tf_op jit(solution)/shard_map/ppermute | solution.py:26
  100.1 33.6 %collective-permute-start.37 = (bf16[128,768]{1,0:T(8,128)(2,1)}, bf16[128,768]{1,0:T(8,128)(2,1)S(1)}, u32[]{:S(2)}, u32[]{:S(2)}) collective-permute-start(bf16[128,768]{1,0:T(8,128)(2,1)} %param.20), channel_id=1, source_target_pairs={{0,8},{8,0},{16,24},{24,16},{1,9},{9,1},{17,25},{25,17},{2,10},{10... | collective-permute-start | bytes 589832 | tf_op jit(solution)/shard_map/ppermute | solution.py:17
  103.2 32.6 %collective-permute-start.38 = (bf16[128,768]{1,0:T(8,128)(2,1)}, bf16[128,768]{1,0:T(8,128)(2,1)S(1)}, u32[]{:S(2)}, u32[]{:S(2)}) collective-permute-start(bf16[128,768]{1,0:T(8,128)(2,1)} %param.20), channel_id=1, source_target_pairs={{0,16},{8,24},{16,0},{24,8},{1,17},{9,25},{17,1},{25,9},{2,18},{10... | collective-permute-start | bytes 589832 | tf_op jit(solution)/shard_map/ppermute | solution.py:17
  106.8 30.3 %collective-permute-start.39 = (bf16[128,768]{1,0:T(8,128)(2,1)}, bf16[128,768]{1,0:T(8,128)(2,1)S(1)}, u32[]{:S(2)}, u32[]{:S(2)}) collective-permute-start(bf16[128,768]{1,0:T(8,128)(2,1)} %param.20), channel_id=1, source_target_pairs={{0,24},{8,16},{16,8},{24,0},{1,25},{9,17},{17,9},{25,1},{2,26},{10... | collective-permute-start | bytes 589832 | tf_op jit(solution)/shard_map/ppermute | solution.py:17
  109.9 100.0 %collective-permute-start.96 = (bf16[128,1536]{1,0:T(8,128)(2,1)S(1)}, bf16[128,1536]{1,0:T(8,128)(2,1)S(1)}, u32[]{:S(2)}, u32[]{:S(2)}) collective-permute-start(bf16[128,1536]{1,0:T(8,128)(2,1)S(1)} %copy-done.56), channel_id=1, source_target_pairs={{0,8},{8,0},{16,24},{24,16},{1,9},{9,1},{17,25},{25,17},{2,10},{10... | collective-permute-start | bytes 1179656 | tf_op jit(solution)/shard_map/ppermute | solution.py:17
  131.5 80.6 %collective-permute-start.97 = (bf16[128,1536]{1,0:T(8,128)(2,1)S(1)}, bf16[128,1536]{1,0:T(8,128)(2,1)S(1)}, u32[]{:S(2)}, u32[]{:S(2)}) collective-permute-start(bf16[128,1536]{1,0:T(8,128)(2,1)S(1)} %copy-done.56), channel_id=1, source_target_pairs={{0,16},{8,24},{16,0},{24,8},{1,17},{9,25},{17,1},{25,9},{2,18},{10... | collective-permute-start | bytes 1179656 | tf_op jit(solution)/shard_map/ppermute | solution.py:17
  133.7 80.7 %collective-permute-start.98 = (bf16[128,1536]{1,0:T(8,128)(2,1)S(1)}, bf16[128,1536]{1,0:T(8,128)(2,1)S(1)}, u32[]{:S(2)}, u32[]{:S(2)}) collective-permute-start(bf16[128,1536]{1,0:T(8,128)(2,1)S(1)} %copy-done.56), channel_id=1, source_target_pairs={{0,24},{8,16},{16,8},{24,0},{1,25},{9,17},{17,9},{25,1},{2,26},{10... | collective-permute-start | bytes 1179656 | tf_op jit(solution)/shard_map/ppermute | solution.py:17
  137.1 140.3 %collective-permute-start.86 = (bf16[192,1536]{1,0:T(8,128)(2,1)}, bf16[192,1536]{1,0:T(8,128)(2,1)}, u32[]{:S(2)}, u32[]{:S(2)}) collective-permute-start(bf16[192,1536]{1,0:T(8,128)(2,1)} %param.31), channel_id=1, source_target_pairs={{0,1},{1,0},{2,3},{3,2},{4,5},{5,4},{6,7},{7,6},{8,9},{9,8},{10,11... | collective-permute-start | bytes 1769480 | tf_op jit(solution)/shard_map/ppermute | solution.py:21
  209.2 70.2 %collective-permute-start.87 = (bf16[192,1536]{1,0:T(8,128)(2,1)}, bf16[192,1536]{1,0:T(8,128)(2,1)}, u32[]{:S(2)}, u32[]{:S(2)}) collective-permute-start(bf16[192,1536]{1,0:T(8,128)(2,1)} %param.31), channel_id=1, source_target_pairs={{0,2},{1,3},{2,4},{3,5},{4,6},{5,7},{6,0},{7,1},{8,10},{9,11},{10,... | collective-permute-start | bytes 1769480 | tf_op jit(solution)/shard_map/ppermute | solution.py:26
  222.2 53.4 %collective-permute-start.17 = (bf16[4,48,1152]{2,1,0:T(8,128)(2,1)}, bf16[4,48,1152]{2,1,0:T(8,128)(2,1)S(1)}, u32[]{:S(2)}, u32[]{:S(2)}) collective-permute-start(bf16[4,48,1152]{2,1,0:T(8,128)(2,1)} %constant_dynamic-update-slice_fusion.33), channel_id=1, source_target_pairs={{0,1},{1,0},{2,3},{3,2},{4,5},{5,4},{6,7},{7,6},{8,9},{9,8},{10,11... | collective-permute-start | bytes 1327112 | tf_op jit(solution)/shard_map/ppermute | solution.py:21
  230.9 44.8 %collective-permute-start.18 = (bf16[4,48,1152]{2,1,0:T(8,128)(2,1)}, bf16[4,48,1152]{2,1,0:T(8,128)(2,1)}, u32[]{:S(2)}, u32[]{:S(2)}) collective-permute-start(bf16[4,48,1152]{2,1,0:T(8,128)(2,1)} %constant_dynamic-update-slice_fusion.33), channel_id=1, source_target_pairs={{0,2},{1,3},{2,4},{3,5},{4,6},{5,7},{6,0},{7,1},{8,10},{9,11},{10,... | collective-permute-start | bytes 1327112 | tf_op jit(solution)/shard_map/ppermute | solution.py:26
  275.0 63.8 %collective-permute-start.79 = (bf16[4,48,3072]{2,1,0:T(8,128)(2,1)}, bf16[4,48,3072]{2,1,0:T(8,128)(2,1)}, u32[]{:S(2)}, u32[]{:S(2)}) collective-permute-start(bf16[4,48,3072]{2,1,0:T(8,128)(2,1)} %constant_dynamic-update-slice_fusion.22), channel_id=1, source_target_pairs={{0,1},{1,0},{2,3},{3,2},{4,5},{5,4},{6,7},{7,6},{8,9},{9,8},{10,11... | collective-permute-start | bytes 3538952 | tf_op jit(solution)/shard_map/ppermute | solution.py:21
  275.7 62.5 %collective-permute-start.80 = (bf16[4,48,3072]{2,1,0:T(8,128)(2,1)}, bf16[4,48,3072]{2,1,0:T(8,128)(2,1)}, u32[]{:S(2)}, u32[]{:S(2)}) collective-permute-start(bf16[4,48,3072]{2,1,0:T(8,128)(2,1)} %constant_dynamic-update-slice_fusion.22), channel_id=1, source_target_pairs={{0,2},{1,3},{2,4},{3,5},{4,6},{5,7},{6,0},{7,1},{8,10},{9,11},{10,... | collective-permute-start | bytes 3538952 | tf_op jit(solution)/shard_map/ppermute | solution.py:26
  283.1 33.0 %collective-permute-start.20 = (bf16[4,48,1152]{2,1,0:T(8,128)(2,1)}, bf16[4,48,1152]{2,1,0:T(8,128)(2,1)}, u32[]{:S(2)}, u32[]{:S(2)}) collective-permute-start(bf16[4,48,1152]{2,1,0:T(8,128)(2,1)} %collective-permute-done.18), channel_id=1, source_target_pairs={{0,2},{1,3},{2,4},{3,5},{4,6},{5,7},{6,0},{7,1},{8,10},{9,11},{10,... | collective-permute-start | bytes 1327112 | tf_op jit(solution)/shard_map/ppermute | solution.py:26
  291.6 26.5 %collective-permute-start.88 = (bf16[192,1536]{1,0:T(8,128)(2,1)}, bf16[192,1536]{1,0:T(8,128)(2,1)S(1)}, u32[]{:S(2)}, u32[]{:S(2)}) collective-permute-start(bf16[192,1536]{1,0:T(8,128)(2,1)} %collective-permute-done.87), channel_id=1, source_target_pairs={{0,1},{1,0},{2,3},{3,2},{4,5},{5,4},{6,7},{7,6},{8,9},{9,8},{10,11... | collective-permute-start | bytes 1769480 | tf_op jit(solution)/shard_map/ppermute | solution.py:21
  295.6 33.0 %collective-permute-start.89 = (bf16[192,1536]{1,0:T(8,128)(2,1)}, bf16[192,1536]{1,0:T(8,128)(2,1)}, u32[]{:S(2)}, u32[]{:S(2)}) collective-permute-start(bf16[192,1536]{1,0:T(8,128)(2,1)} %collective-permute-done.87), channel_id=1, source_target_pairs={{0,2},{1,3},{2,4},{3,5},{4,6},{5,7},{6,0},{7,1},{8,10},{9,11},{10,... | collective-permute-start | bytes 1769480 | tf_op jit(solution)/shard_map/ppermute | solution.py:26
  331.5 28.3 %collective-permute-start.91 = (bf16[192,1536]{1,0:T(8,128)(2,1)}, bf16[192,1536]{1,0:T(8,128)(2,1)}, u32[]{:S(2)}, u32[]{:S(2)}) collective-permute-start(bf16[192,1536]{1,0:T(8,128)(2,1)} %collective-permute-done.89), channel_id=1, source_target_pairs={{0,2},{1,3},{2,4},{3,5},{4,6},{5,7},{6,0},{7,1},{8,10},{9,11},{10,... | collective-permute-start | bytes 1769480 | tf_op jit(solution)/shard_map/ppermute | solution.py:26
  338.2 71.9 %collective-permute-start.81 = (bf16[4,48,3072]{2,1,0:T(8,128)(2,1)}, bf16[4,48,3072]{2,1,0:T(8,128)(2,1)}, u32[]{:S(2)}, u32[]{:S(2)}) collective-permute-start(bf16[4,48,3072]{2,1,0:T(8,128)(2,1)} %collective-permute-done.80), channel_id=1, source_target_pairs={{0,1},{1,0},{2,3},{3,2},{4,5},{5,4},{6,7},{7,6},{8,9},{9,8},{10,11... | collective-permute-start | bytes 3538952 | tf_op jit(solution)/shard_map/ppermute | solution.py:21
  338.7 45.8 %collective-permute-start.82 = (bf16[4,48,3072]{2,1,0:T(8,128)(2,1)}, bf16[4,48,3072]{2,1,0:T(8,128)(2,1)}, u32[]{:S(2)}, u32[]{:S(2)}) collective-permute-start(bf16[4,48,3072]{2,1,0:T(8,128)(2,1)} %collective-permute-done.80), channel_id=1, source_target_pairs={{0,2},{1,3},{2,4},{3,5},{4,6},{5,7},{6,0},{7,1},{8,10},{9,11},{10,... | collective-permute-start | bytes 3538952 | tf_op jit(solution)/shard_map/ppermute | solution.py:26
  384.6 70.6 %collective-permute-start.83 = (bf16[4,48,3072]{2,1,0:T(8,128)(2,1)}, bf16[4,48,3072]{2,1,0:T(8,128)(2,1)}, u32[]{:S(2)}, u32[]{:S(2)}) collective-permute-start(bf16[4,48,3072]{2,1,0:T(8,128)(2,1)} %collective-permute-done.82), channel_id=1, source_target_pairs={{0,1},{1,0},{2,3},{3,2},{4,5},{5,4},{6,7},{7,6},{8,9},{9,8},{10,11... | collective-permute-start | bytes 3538952 | tf_op jit(solution)/shard_map/ppermute | solution.py:21
  392.1 63.0 %collective-permute-start.84 = (bf16[4,48,3072]{2,1,0:T(8,128)(2,1)}, bf16[4,48,3072]{2,1,0:T(8,128)(2,1)}, u32[]{:S(2)}, u32[]{:S(2)}) collective-permute-start(bf16[4,48,3072]{2,1,0:T(8,128)(2,1)} %collective-permute-done.82), channel_id=1, source_target_pairs={{0,2},{1,3},{2,4},{3,5},{4,6},{5,7},{6,0},{7,1},{8,10},{9,11},{10,... | collective-permute-start | bytes 3538952 | tf_op jit(solution)/shard_map/ppermute | solution.py:26
  505.2 27.4 %collective-permute-start.101 = (bf16[128,1536]{1,0:T(8,128)(2,1)}, bf16[128,1536]{1,0:T(8,128)(2,1)}, u32[]{:S(2)}, u32[]{:S(2)}) collective-permute-start(bf16[128,1536]{1,0:T(8,128)(2,1)} %get-tuple-element.59), channel_id=1, source_target_pairs={{0,24},{8,16},{16,8},{24,0},{1,25},{9,17},{17,9},{25,1},{2,26},{10... | collective-permute-start | bytes 1179656 | tf_op jit(solution)/shard_map/ppermute | solution.py:17
  506.8 33.6 %collective-permute-start.100 = (bf16[128,1536]{1,0:T(8,128)(2,1)}, bf16[128,1536]{1,0:T(8,128)(2,1)}, u32[]{:S(2)}, u32[]{:S(2)}) collective-permute-start(bf16[128,1536]{1,0:T(8,128)(2,1)} %get-tuple-element.60), channel_id=1, source_target_pairs={{0,16},{8,24},{16,0},{24,8},{1,17},{9,25},{17,1},{25,9},{2,18},{10... | collective-permute-start | bytes 1179656 | tf_op jit(solution)/shard_map/ppermute | solution.py:17
  508.2 32.3 %collective-permute-start.99 = (bf16[128,1536]{1,0:T(8,128)(2,1)}, bf16[128,1536]{1,0:T(8,128)(2,1)}, u32[]{:S(2)}, u32[]{:S(2)}) collective-permute-start(bf16[128,1536]{1,0:T(8,128)(2,1)} %get-tuple-element.58), channel_id=1, source_target_pairs={{0,8},{8,0},{16,24},{24,16},{1,9},{9,1},{17,25},{25,17},{2,10},{10... | collective-permute-start | bytes 1179656 | tf_op jit(solution)/shard_map/ppermute | solution.py:17
  540.5 272.5 %collective-permute-start.143 = (bf16[4,4,48,3072]{3,2,1,0:T(8,128)(2,1)}, bf16[4,4,48,3072]{3,2,1,0:T(8,128)(2,1)}, u32[]{:S(2)}, u32[]{:S(2)}) collective-permute-start(bf16[4,4,48,3072]{3,2,1,0:T(8,128)(2,1)} %bitcast.813), channel_id=1, source_target_pairs={{0,1},{1,0},{2,3},{3,2},{4,5},{5,4},{6,7},{7,6},{8,9},{9,8},{10,11... | collective-permute-start | bytes 14155784 | tf_op jit(solution)/shard_map/ppermute | solution.py:21
  552.6 190.7 %collective-permute-start.155 = (bf16[4,192,1536]{2,1,0:T(8,128)(2,1)}, bf16[4,192,1536]{2,1,0:T(8,128)(2,1)}, u32[]{:S(2)}, u32[]{:S(2)}) collective-permute-start(bf16[4,192,1536]{2,1,0:T(8,128)(2,1)} %dynamic-slice_bitcast_fusion), channel_id=1, source_target_pairs={{0,1},{1,0},{2,3},{3,2},{4,5},{5,4},{6,7},{7,6},{8,9},{9,8},{10,11... | collective-permute-start | bytes 7077896 | tf_op jit(solution)/shard_map/ppermute | solution.py:21
  609.2 26.8 %collective-permute-start.108 = (bf16[128,1536]{1,0:T(8,128)(2,1)S(1)}, bf16[128,1536]{1,0:T(8,128)(2,1)S(1)}, u32[]{:S(2)}, u32[]{:S(2)}) collective-permute-start(bf16[128,1536]{1,0:T(8,128)(2,1)S(1)} %get-tuple-element.24), channel_id=1, source_target_pairs={{0,8},{8,0},{16,24},{24,16},{1,9},{9,1},{17,25},{25,17},{2,10},{10... | collective-permute-start | bytes 1179656 | tf_op jit(solution)/shard_map/ppermute | solution.py:17
  611.7 24.3 %collective-permute-start.109 = (bf16[128,1536]{1,0:T(8,128)(2,1)S(1)}, bf16[128,1536]{1,0:T(8,128)(2,1)S(1)}, u32[]{:S(2)}, u32[]{:S(2)}) collective-permute-start(bf16[128,1536]{1,0:T(8,128)(2,1)S(1)} %get-tuple-element.24), channel_id=1, source_target_pairs={{0,16},{8,24},{16,0},{24,8},{1,17},{9,25},{17,1},{25,9},{2,18},{10... | collective-permute-start | bytes 1179656 | tf_op jit(solution)/shard_map/ppermute | solution.py:17
  636.0 40.4 %collective-permute-start.127 = (bf16[4,48,384]{2,1,0:T(8,128)(2,1)}, bf16[4,48,384]{2,1,0:T(8,128)(2,1)}, u32[]{:S(2)}, u32[]{:S(2)}) collective-permute-start(bf16[4,48,384]{2,1,0:T(8,128)(2,1)} %fusion.109), channel_id=1, source_target_pairs={{0,2},{1,3},{2,4},{3,5},{4,6},{5,7},{6,0},{7,1},{8,10},{9,11},{10,... | collective-permute-start | bytes 442376 | tf_op jit(solution)/shard_map/ppermute | solution.py:26
  636.0 41.8 %collective-permute-start.134 = (bf16[4,24,768]{2,1,0:T(8,128)(2,1)}, bf16[4,24,768]{2,1,0:T(8,128)(2,1)}, u32[]{:S(2)}, u32[]{:S(2)}) collective-permute-start(bf16[4,24,768]{2,1,0:T(8,128)(2,1)} %fusion.106), channel_id=1, source_target_pairs={{0,2},{1,3},{2,4},{3,5},{4,6},{5,7},{6,0},{7,1},{8,10},{9,11},{10,... | collective-permute-start | bytes 442376 | tf_op jit(solution)/shard_map/ppermute | solution.py:26
  643.0 31.0 %collective-permute-start.141 = (bf16[48,1536]{1,0:T(8,128)(2,1)}, bf16[48,1536]{1,0:T(8,128)(2,1)}, u32[]{:S(2)}, u32[]{:S(2)}) collective-permute-start(bf16[48,1536]{1,0:T(8,128)(2,1)} %fusion.104), channel_id=1, source_target_pairs={{0,2},{1,3},{2,4},{3,5},{4,6},{5,7},{6,0},{7,1},{8,10},{9,11},{10,... | collective-permute-start | bytes 442376 | tf_op jit(solution)/shard_map/ppermute | solution.py:26
  674.0 56.6 %collective-permute-start.113 = (bf16[128,1536]{1,0:T(8,128)(2,1)S(1)}, bf16[128,1536]{1,0:T(8,128)(2,1)S(1)}, u32[]{:S(2)}, u32[]{:S(2)}) collective-permute-start(bf16[128,1536]{1,0:T(8,128)(2,1)S(1)} %get-tuple-element.53), channel_id=1, source_target_pairs={{0,24},{8,16},{16,8},{24,0},{1,25},{9,17},{17,9},{25,1},{2,26},{10... | collective-permute-start | bytes 1179656 | tf_op jit(solution)/shard_map/ppermute | solution.py:17
  676.4 54.4 %collective-permute-start.112 = (bf16[128,1536]{1,0:T(8,128)(2,1)S(1)}, bf16[128,1536]{1,0:T(8,128)(2,1)S(1)}, u32[]{:S(2)}, u32[]{:S(2)}) collective-permute-start(bf16[128,1536]{1,0:T(8,128)(2,1)S(1)} %get-tuple-element.54), channel_id=1, source_target_pairs={{0,16},{8,24},{16,0},{24,8},{1,17},{9,25},{17,1},{25,9},{2,18},{10... | collective-permute-start | bytes 1179656 | tf_op jit(solution)/shard_map/ppermute | solution.py:17
  751.5 25.4 %collective-permute-start.124 = (bf16[48,1536]{1,0:T(8,128)(2,1)S(1)}, bf16[48,1536]{1,0:T(8,128)(2,1)S(1)}, u32[]{:S(2)}, u32[]{:S(2)}) collective-permute-start(bf16[48,1536]{1,0:T(8,128)(2,1)S(1)} %fusion.113), channel_id=1, source_target_pairs={{0,2},{1,3},{2,4},{3,5},{4,6},{5,7},{6,0},{7,1},{8,10},{9,11},{10,... | collective-permute-start | bytes 442376 | tf_op jit(solution)/shard_map/ppermute | solution.py:26
  752.2 24.6 %collective-permute-start.115 = (bf16[4,48,1152]{2,1,0:T(8,128)(2,1)S(1)}, bf16[4,48,1152]{2,1,0:T(8,128)(2,1)S(1)}, u32[]{:S(2)}, u32[]{:S(2)}) collective-permute-start(bf16[4,48,1152]{2,1,0:T(8,128)(2,1)S(1)} %dynamic-slice_bitcast_fusion.5), channel_id=1, source_target_pairs={{0,2},{1,3},{2,4},{3,5},{4,6},{5,7},{6,0},{7,1},{8,10},{9,11},{10,... | collective-permute-start | bytes 1327112 | tf_op jit(solution)/shard_map/ppermute | solution.py:26
  764.3 33.5 %collective-permute-start.157 = (bf16[192,1536]{1,0:T(8,128)(2,1)S(1)}, bf16[192,1536]{1,0:T(8,128)(2,1)S(1)}, u32[]{:S(2)}, u32[]{:S(2)}) collective-permute-start(bf16[192,1536]{1,0:T(8,128)(2,1)S(1)} %fusion.34), channel_id=1, source_target_pairs={{0,2},{1,3},{2,4},{3,5},{4,6},{5,7},{6,0},{7,1},{8,10},{9,11},{10,... | collective-permute-start | bytes 1769480 | tf_op jit(solution)/shard_map/ppermute | solution.py:26
  798.0 27.4 %collective-permute-start.158 = (bf16[192,1536]{1,0:T(8,128)(2,1)S(1)}, bf16[192,1536]{1,0:T(8,128)(2,1)S(1)}, u32[]{:S(2)}, u32[]{:S(2)}) collective-permute-start(bf16[192,1536]{1,0:T(8,128)(2,1)S(1)} %fusion.35), channel_id=1, source_target_pairs={{0,2},{1,3},{2,4},{3,5},{4,6},{5,7},{6,0},{7,1},{8,10},{9,11},{10,... | collective-permute-start | bytes 1769480 | tf_op jit(solution)/shard_map/ppermute | solution.py:26
  817.5 31.0 %collective-permute-start.144 = (bf16[4,48,3072]{2,1,0:T(8,128)(2,1)S(1)}, bf16[4,48,3072]{2,1,0:T(8,128)(2,1)S(1)}, u32[]{:S(2)}, u32[]{:S(2)}) collective-permute-start(bf16[4,48,3072]{2,1,0:T(8,128)(2,1)S(1)} %dynamic-slice_bitcast_fusion.1), channel_id=1, source_target_pairs={{0,2},{1,3},{2,4},{3,5},{4,6},{5,7},{6,0},{7,1},{8,10},{9,11},{10,... | collective-permute-start | bytes 3538952 | tf_op jit(solution)/shard_map/ppermute | solution.py:26
  848.9 27.6 %collective-permute-start.145 = (bf16[4,48,3072]{2,1,0:T(8,128)(2,1)S(1)}, bf16[4,48,3072]{2,1,0:T(8,128)(2,1)S(1)}, u32[]{:S(2)}, u32[]{:S(2)}) collective-permute-start(bf16[4,48,3072]{2,1,0:T(8,128)(2,1)S(1)} %fusion.7), channel_id=1, source_target_pairs={{0,2},{1,3},{2,4},{3,5},{4,6},{5,7},{6,0},{7,1},{8,10},{9,11},{10,... | collective-permute-start | bytes 3538952 | tf_op jit(solution)/shard_map/ppermute | solution.py:26
  876.9 26.7 %collective-permute-start.146 = (bf16[4,48,3072]{2,1,0:T(8,128)(2,1)S(1)}, bf16[4,48,3072]{2,1,0:T(8,128)(2,1)S(1)}, u32[]{:S(2)}, u32[]{:S(2)}) collective-permute-start(bf16[4,48,3072]{2,1,0:T(8,128)(2,1)S(1)} %fusion.8), channel_id=1, source_target_pairs={{0,2},{1,3},{2,4},{3,5},{4,6},{5,7},{6,0},{7,1},{8,10},{9,11},{10,... | collective-permute-start | bytes 3538952 | tf_op jit(solution)/shard_map/ppermute | solution.py:26
  (228 other events, 2292.8 us)
